TPU v7x, 32 devices: a whole 2x2x4 slice. The times are simulated.
32 devices in a mesh: mem: 4 (over y, x), tile: 4 (over z), grp: 2 (over core).
Axes of the slice: x: 2, y: 2, z: 4, core: 2. Of those that a mesh axis runs over, the one named last changes fastest.
Arguments:
- members: float32 [3, 128, 64, 512], P(None, 'mem', ('tile', 'grp')), may hold values from -0.6 to 0.6
- obs_cells: int32 [8, 4, 1024], P(('tile', 'grp'), 'mem'), may hold values from 0 to 1023
- obs_count: int32 [8, 4], P(('tile', 'grp'), 'mem'), may hold values from 128 to 1024, as said below
- obs_values: float32 [8, 4, 1024], P(('tile', 'grp'), 'mem'), may hold values from -0.6 to 0.6
- obs_error: float32 [8, 4, 1024], P(('tile', 'grp'), 'mem'), may hold values from 0.03 to 0.3
- obs_noise: float32 [8, 4, 1024, 128], P(('tile', 'grp'), 'mem'), may hold values from -6 to 6
Outputs:
- analysis: bfloat16 [3, 128, 64, 512], P(None, None, ('tile', 'grp'), 'mem')
Inputs may be any that keep to these rules, and one draw needn't show every extreme that they name: `obs_count`: a multiple of 128; some tile has exactly 1024 live slots in every draw.
All inputs are finite; a program needn't handle non-finite values.
Results may differ from a plain program's by a relative error of at most 0.0058.
Values may be sent and summed in bfloat16 or wider, within the bound.
A program may use at most 64 MiB of HBM per device.

v0:
```python
import jax
import jax.numpy as jnp
from jax import lax
from jax.experimental import pallas as pl
from jax.experimental.pallas import tpu as pltpu
from jax.sharding import PartitionSpec as P

STEPS = 4
NEWTON_STEPS = 13

courant = 0.3
gravity = 1.0
coriolis = 0.1
VMEM_BYTES = 60000000
MESH = pl.DeviceIdType.MESH


def advance(west, mid, east):
    (hw, uw, vw), (h, u, v), (he, ue, ve) = west, mid, east
    cols = h.shape[1]
    north = lambda q: pltpu.roll(q, cols - 1, 1)
    south = lambda q: pltpu.roll(q, 1, 1)
    hn, hs, un, us, vn, vs = north(h), south(h), north(u), south(u), north(v), south(v)
    new_h = (
        0.25 * (he + hw + hn + hs)
        - courant * ((1.0 + he) * ue - (1.0 + hw) * uw)
        - courant * ((1.0 + hn) * vn - (1.0 + hs) * vs)
    )
    new_u = (
        0.25 * (ue + uw + un + us)
        - courant * ((0.5 * ue * ue + gravity * he) - (0.5 * uw * uw + gravity * hw))
        - courant * v * (un - us)
        + coriolis * v
    )
    new_v = (
        0.25 * (ve + vw + vn + vs)
        - courant * ((0.5 * vn * vn + gravity * hn) - (0.5 * vs * vs + gravity * hs))
        - courant * u * (ve - vw)
        - coriolis * u
    )
    return new_h, new_u, new_v


def split(q):
    high = q.astype(jnp.bfloat16)
    rest = q - high.astype(jnp.float32)
    middle = rest.astype(jnp.bfloat16)
    return high, middle, (rest - middle.astype(jnp.float32)).astype(jnp.bfloat16)


def mxu(a, b):
    return jnp.dot(a, b, preferred_element_type=jnp.float32)


def product(a, b):
    (ah, am, al), (bh, bm, bl) = a, b
    size = bh.shape[1]
    top = mxu(
        jnp.concatenate([ah, am], axis=1),
        jnp.concatenate([jnp.concatenate([bh, bm], axis=1)] * 2, axis=0),
    )
    low = mxu(jnp.concatenate([ah, al], axis=1), jnp.concatenate([bl, bh], axis=0))
    return top[:, :size] + (top[:, size:] + low)


def solve_turned(gram, rhs, least):
    size = gram.shape[0]
    bound = jnp.max(jnp.sum(jnp.abs(gram), axis=0, keepdims=True), axis=1, keepdims=True)
    bound = jnp.broadcast_to(bound, (1, size))
    scale = 1.0 / bound
    eye = jnp.where(
        lax.broadcasted_iota(jnp.int32, (size, size), 0) == lax.broadcasted_iota(jnp.int32, (size, size), 1), 1.0, 0.0
    )
    low = least * scale
    y, x = gram * scale, eye * scale
    for _ in range(NEWTON_STEPS):
        mid = 1.0 + low
        gain = 4.0 / (mid * mid)
        low = gain * low
        parts = split(y)
        both = [jnp.concatenate(pair, axis=0) for pair in zip(parts, split(x))]
        done = product(both, parts)
        y = gain * (mid * y - done[:size])
        x = gain * (mid * x - done[size:])
    inverse = split(x)
    found = product(split(rhs), inverse)
    rest = rhs - product(split(found), split(gram))
    return found + product(split(rest), inverse), eye


def neighbour_ids():
    groups = lax.axis_size("grp")
    total = lax.axis_size("tile") * groups
    me = lax.axis_index("tile") * groups + lax.axis_index("grp")
    after, before = lax.rem(me + 1, total), lax.rem(me + total - 1, total)
    return [{"tile": i // groups, "grp": lax.rem(i, groups)} for i in (after, before)]


def kernel(
    members_hbm, count_hbm, cells_hbm, values_hbm, error_hbm, noise_hbm, out_hbm,
    lev, edges, halo, ready, recv, noise, cells, values, error, count, pick, target, observed, tall, packed,
    row_sem, load_sem, halo_send, halo_recv, part_send, part_recv, own_sem, out_sem,
):
    fields, ens, rows, cols = members_hbm.shape
    waves = rows
    assert rows == 2 * STEPS
    lines = rows + 2 * STEPS
    parts, tile_cols = ready.shape[1], ready.shape[4]
    full = parts * ens
    slots = cells.shape[1]
    me = lax.axis_index("mem")
    after, before = neighbour_ids()
    peers = [lax.rem(me + p, parts) for p in range(1, parts)]
    targets = [after, before] + [{"mem": p} for p in peers]
    quick = 1 - lax.rem(lax.axis_index("grp"), 2)

    def row_load(r):
        return pltpu.make_async_copy(members_hbm.at[:, :, r, :], lev.at[STEPS + r], row_sem.at[r])

    small = [
        pltpu.make_async_copy(src, dst, load_sem.at[i])
        for i, (src, dst) in enumerate(
            ((noise_hbm, noise), (cells_hbm, cells), (values_hbm, values), (error_hbm, error), (count_hbm, count))
        )
    ]
    for k in range(STEPS):
        row_load(rows - 1 - k).start()
        row_load(k).start()
    for load in small:
        load.start()
    barrier = pltpu.get_barrier_semaphore()
    for target_id in targets:
        pl.semaphore_signal(barrier, inc=1, device_id=target_id, device_id_type=MESH)

    def halo_copy(way, k):
        return pltpu.make_async_remote_copy(
            src_ref=edges.at[way, k],
            dst_ref=halo.at[way, k],
            send_sem=halo_send.at[way, k],
            recv_sem=halo_recv.at[way, k],
            device_id=(after, before)[way],
            device_id_type=MESH,
        )

    for k in range(STEPS):
        for way, r in ((0, rows - 1 - k), (1, k)):
            row_load(r).wait()
            edges[way, k] = lev[STEPS + r].astype(jnp.bfloat16)
        if k == 0:
            pl.semaphore_wait(barrier, len(targets))
        for way in range(2):
            halo_copy(way, k).start()

    def stencil(base, half):
        def at(i):
            return [lev[i, f, pl.ds(half, 8), :] for f in range(fields)]

        return advance(at(base - 1), at(base), at(base + 1))

    def step_row(level, line):
        base = level * lines + line
        for half in range(0, ens, 8):
            done = stencil(base, half)
            for f in range(fields):
                lev[base + lines, f, pl.ds(half, 8), :] = done[f]

    for level in range(STEPS - 1):

        def inner_row(i, carry, level=level):
            step_row(level, STEPS + level + 1 + i)
            return carry

        lax.fori_loop(0, rows - 2 * (level + 1), inner_row, 0)

    def wave_side(w):
        late = w // STEPS
        return quick + late - 2 * quick * late, lax.rem(w, STEPS)

    def wave_row(w):
        side, k = wave_side(w)
        return (STEPS - 1 - k) + side * (2 * k + 1)

    def part_copy(w, kind, p):
        f, number = ((0, 1), (1, fields - 1))[kind]
        return pltpu.make_async_remote_copy(
            src_ref=ready.at[w, peers[p], pl.ds(f, number)],
            dst_ref=recv.at[w, pl.ds(f, number), pl.ds(me * ens, ens)],
            send_sem=part_send.at[w, kind, p],
            recv_sem=part_recv.at[w, kind, p],
            device_id={"mem": peers[p]},
            device_id_type=MESH,
        )

    def own_copy(w):
        return pltpu.make_async_copy(ready.at[w, me], recv.at[w, :, pl.ds(me * ens, ens)], own_sem.at[w])

    def wave(w, carry):
        side, k = wave_side(w)
        sign = 1 - 2 * side
        start = (STEPS - 1 - k) + side * (2 * k + lines - 2 * STEPS + 1)
        pltpu.make_async_copy(halo.at[side, k], halo.at[side, k], halo_recv.at[side, k]).wait()
        lev[start] = halo[side, k].astype(jnp.float32)

        def up(level, c):
            step_row(level, start + sign * (level + 1))
            return c

        lax.fori_loop(0, STEPS - 1, up, 0)
        base = (STEPS - 1) * lines + start + sign * STEPS
        for m in range(0, ens, 16):
            pair = [stencil(base, m), stencil(base, m + 8)]
            for f in range(fields):
                both = jnp.concatenate([pair[0][f], pair[1][f]], axis=0).astype(jnp.bfloat16)
                for d in range(parts):
                    ready[w, d, f, pl.ds(m, 16), :] = both[:, d * tile_cols : (d + 1) * tile_cols]
        for kind in range(2):
            for p in range(parts - 1):
                part_copy(w, kind, p).start()
        own_copy(w).start()
        return carry

    lax.fori_loop(0, STEPS, wave, 0)

    for load in small:
        load.wait()

    def select(w, carry):
        ids = lax.broadcasted_iota(jnp.int32, (tile_cols, slots), 0) + wave_row(w) * tile_cols
        pick[pl.ds(pl.multiple_of(w * tile_cols, tile_cols), tile_cols), :] = jnp.where(
            ids == cells[...], 1.0, 0.0
        ).astype(jnp.bfloat16)
        return carry

    lax.fori_loop(0, waves, select, 0)
    chunk = 256 if slots % 256 == 0 else slots
    for s in range(0, slots, chunk):
        cut = slice(s, s + chunk)
        for i, third in enumerate(split(values[:, cut] + error[:, cut] * noise[cut, :].T)):
            target[i, :, cut] = third

    lax.fori_loop(STEPS, waves, wave, 0)

    def arrived(w):
        own_copy(w).wait()
        for p in range(parts - 1):
            part_copy(w, 0, p).wait_recv()

    def look(first, number, cut):
        seen = jnp.concatenate([recv[w, 0] for w in range(first, first + number)], axis=1)
        return mxu(seen, pick[first * tile_cols : (first + number) * tile_cols, cut])

    early = waves - 1
    for w in range(early):
        arrived(w)
    for s in range(0, slots, chunk):
        observed[:, s : s + chunk] = look(0, early, slice(s, s + chunk))
    arrived(early)
    slot_ids = lax.broadcasted_iota(jnp.int32, (1, slots), 1)
    weights = jnp.where(slot_ids < count[...], 1.0 / (error[...] * error[...]), 0.0)
    both = None
    for s in range(0, slots, chunk):
        cut = slice(s, s + chunk)
        yb = observed[:, cut] + look(early, 1, cut)
        spread = yb - jnp.sum(yb, axis=0, keepdims=True) * (1.0 / full)
        wh, wm, wl = split(spread * weights[:, cut])
        yb = yb.astype(jnp.bfloat16)
        dh, dm, dl = (target[i, :, cut] for i in range(3))

        def turned(a, b):
            return lax.dot_general(a, b, (((1,), (1,)), ((), ())), preferred_element_type=jnp.float32)

        one = turned(jnp.concatenate([yb, dh, dm], axis=0), jnp.concatenate([wh, wm], axis=0))
        two = turned(jnp.concatenate([yb, dh], axis=0), wl)
        three = turned(dl, wh)
        term = [one[:full, :full], one[:full, full:] + two[:full]]
        term += [one[full : 2 * full, :full]]
        term += [one[full : 2 * full, full:] + one[2 * full :, :full] + one[2 * full :, full:] + two[full:] + three]
        both = term if both is None else [a + b for a, b in zip(both, term)]
    plain = both[0] + both[1]
    aimed = both[2] + both[3]
    least = full - 1.0
    eye = jnp.where(
        lax.broadcasted_iota(jnp.int32, (full, full), 0) == lax.broadcasted_iota(jnp.int32, (full, full), 1), 1.0, 0.0
    )
    gram = plain - jnp.sum(plain, axis=0, keepdims=True) * (1.0 / full) + least * eye
    rhs = aimed - plain
    rhs = rhs - jnp.sum(rhs, axis=1, keepdims=True) * (1.0 / full)
    solved, eye = solve_turned(gram, rhs, least)
    mix = solved + eye
    upper = mix.astype(jnp.bfloat16)
    lower = (mix - upper.astype(jnp.float32)).astype(jnp.bfloat16)
    mix = jnp.concatenate([upper, lower], axis=1)
    for f in range(fields):
        for w in range(0, waves, 2):
            if f == 1:
                for i in (w, w + 1):
                    for p in range(parts - 1):
                        part_copy(i, 1, p).wait_recv()
            block = jnp.concatenate([recv[w, f], recv[w + 1, f]], axis=1)
            done = mxu(mix, jnp.concatenate([block, block], axis=0))
            for i in range(2):
                tall[f, pl.ds(wave_row(w + i), full, stride=rows), :] = done[:, i * tile_cols : (i + 1) * tile_cols]
        packed[f] = tall[f].reshape(full, rows, tile_cols).astype(jnp.bfloat16)
        pltpu.make_async_copy(packed.at[f], out_hbm.at[f], out_sem.at[f]).start()
    for way in range(2):
        for k in range(STEPS):
            halo_copy(way, k).wait_send()

    def finish(w, carry):
        for kind in range(2):
            for p in range(parts - 1):
                part_copy(w, kind, p).wait_send()
        return carry

    lax.fori_loop(0, waves, finish, 0)
    for f in range(fields):
        pltpu.make_async_copy(packed.at[f], out_hbm.at[f], out_sem.at[f]).wait()


def hbm():
    return pl.BlockSpec(memory_space=pltpu.HBM)


def body(members, obs_cells, obs_count, obs_values, obs_error, obs_noise):
    fields, ens, rows, cols = members.shape
    parts = lax.axis_size("mem")
    tile_cols = cols // parts
    full = ens * parts
    points = rows * tile_cols
    slots = obs_cells.shape[2]
    lines = rows + 2 * STEPS
    edge = pltpu.VMEM((2, STEPS, fields, ens, cols), jnp.bfloat16)
    row = pltpu.VMEM((1, slots), jnp.float32)
    dma = pltpu.SemaphoreType.DMA
    return pl.pallas_call(
        kernel,
        name="assimilate",
        out_shape=jax.ShapeDtypeStruct((fields, full, rows, tile_cols), jnp.bfloat16),
        in_specs=[hbm()] * 6,
        out_specs=hbm(),
        scratch_shapes=[
            pltpu.VMEM((STEPS * lines, fields, ens, cols), jnp.float32),
            edge,
            edge,
            pltpu.VMEM((rows, parts, fields, ens, tile_cols), jnp.bfloat16),
            pltpu.VMEM((rows, fields, full, tile_cols), jnp.bfloat16),
            pltpu.VMEM(obs_noise.shape[2:], jnp.float32),
            pltpu.VMEM((1, slots), jnp.int32),
            row,
            row,
            pltpu.VMEM((1, 1), jnp.int32),
            pltpu.VMEM((points, slots), jnp.bfloat16),
            pltpu.VMEM((3, full, slots), jnp.bfloat16),
            pltpu.VMEM((full, slots), jnp.float32),
            pltpu.VMEM((fields, full * rows, tile_cols), jnp.float32),
            pltpu.VMEM((fields, full, rows, tile_cols), jnp.bfloat16),
            dma((rows,)),
            dma((5,)),
            dma((2, STEPS)),
            dma((2, STEPS)),
            dma((rows, 2, parts - 1)),
            dma((rows, 2, parts - 1)),
            dma((rows,)),
            dma((fields,)),
        ],
        compiler_params=pltpu.CompilerParams(
            vmem_limit_bytes=VMEM_BYTES, collective_id=0, has_side_effects=True
        ),
    )(members, obs_count, obs_cells[0], obs_values[0], obs_error[0], obs_noise[0, 0])


def solution(mesh):
    in_specs = (
        P(None, "mem", ("tile", "grp"), None),
        P(("tile", "grp"), "mem", None),
        P(("tile", "grp"), "mem"),
        P(("tile", "grp"), "mem", None),
        P(("tile", "grp"), "mem", None),
        P(("tile", "grp"), "mem", None, None),
    )
    out_specs = P(None, None, ("tile", "grp"), "mem")
    return jax.shard_map(body, mesh=mesh, in_specs=in_specs, out_specs=out_specs, check_vma=False)
```

profile of v0, /device:TPU:0, one launch (start us, length us, event | category | flops | bytes accessed | tf_op | source)
XLA Modules:
  0.0 29.6 jit_solution(4115038814439677267)
XLA Ops:
  0.7 26.9 %assimilate.1 = bf16[3,128,8,128]{3,2,1,0:T(8,128)(2,1)} custom-call(f32[3,32,8,512]{3,2,1,0:T(8,128)} %members_hbm.1, s32[1,1]{1,0:T(1,128)S(6)} %copy.8.count_hbm, s32[1,1024]{1,0:T(1,128)} %bitcast.5, f32[1,1024]{1,0:T(1,128)} %bitcast.6, f32[1,1024]{1,0:T(1,128)} %bitcast.7, f32[1024,128]{1,0:T(8,128)} %bitcast.4), custom_call_target="tpu_custom_call" | custom-call | tf_op jit(solution)/shard_map/assimilate/pallas_call | solution.py:335
  27.6 2.1 %copy.9 = bf16[3,128,8,128]{3,2,1,0:T(8,128)(2,1)} copy(bf16[3,128,8,128]{3,2,1,0:T(8,128)(2,1)} %assimilate.1) | data formatting | bytes 1572864
where the time goes:
time: 29.8 us; the launch traced here: 29.6 us
  Pallas kernels  26.9 us (90%)
  local copies, waits for them, and re-layouts  2.06 us (7%)
  between operations  0.66 us (2%)
    pallas_call x1, Pallas kernels, body(): pl.pallas_call(kernel, name='assimilate', out_shape=jax.ShapeDtypeStruct(...  26.9 us
    unnamed x1, local copies, waits for them, and re-layouts  2.06 us

commit v1 on v0

--- a/solution.py
+++ b/solution.py
@@ -6,12 +6,12 @@
 from jax.sharding import PartitionSpec as P
 
 STEPS = 4
-NEWTON_STEPS = 13
+NEWTON_STEPS = 12
 
 courant = 0.3
 gravity = 1.0
 coriolis = 0.1
-VMEM_BYTES = 60000000
+VMEM_BYTES = 45000000
 MESH = pl.DeviceIdType.MESH
 
 
@@ -20,23 +20,22 @@
     cols = h.shape[1]
     north = lambda q: pltpu.roll(q, cols - 1, 1)
     south = lambda q: pltpu.roll(q, 1, 1)
-    hn, hs, un, us, vn, vs = north(h), south(h), north(u), south(u), north(v), south(v)
-    new_h = (
-        0.25 * (he + hw + hn + hs)
-        - courant * ((1.0 + he) * ue - (1.0 + hw) * uw)
-        - courant * ((1.0 + hn) * vn - (1.0 + hs) * vs)
-    )
+    flux = courant * (v + h * v)
+    near = 0.25 * h
+    rise = ue - uw
+    new_h = 0.25 * (he + hw) - courant * (rise + (he * ue - hw * uw)) + (north(near - flux) + south(near + flux))
+    un, us = north(u), south(u)
     new_u = (
-        0.25 * (ue + uw + un + us)
-        - courant * ((0.5 * ue * ue + gravity * he) - (0.5 * uw * uw + gravity * hw))
-        - courant * v * (un - us)
-        + coriolis * v
-    )
+        (ue + uw) * (0.25 - (0.5 * courant) * rise)
+        - (courant * gravity) * (he - hw)
+        + (0.25 * (un + us) + v * (coriolis - courant * (un - us)))
+    )
+    flux = courant * (0.5 * (v * v) + gravity * h)
+    near = 0.25 * v
     new_v = (
-        0.25 * (ve + vw + vn + vs)
-        - courant * ((0.5 * vn * vn + gravity * hn) - (0.5 * vs * vs + gravity * hs))
-        - courant * u * (ve - vw)
-        - coriolis * u
+        0.25 * (ve + vw)
+        - u * (coriolis + courant * (ve - vw))
+        + (north(near - flux) + south(near + flux))
     )
     return new_h, new_u, new_v
 
@@ -88,18 +87,15 @@
     return found + product(split(rest), inverse), eye
 
 
-def neighbour_ids():
+def place_of(slab):
     groups = lax.axis_size("grp")
-    total = lax.axis_size("tile") * groups
-    me = lax.axis_index("tile") * groups + lax.axis_index("grp")
-    after, before = lax.rem(me + 1, total), lax.rem(me + total - 1, total)
-    return [{"tile": i // groups, "grp": lax.rem(i, groups)} for i in (after, before)]
+    return {"tile": slab // groups, "grp": lax.rem(slab, groups)}
 
 
 def kernel(
-    members_hbm, count_hbm, cells_hbm, values_hbm, error_hbm, noise_hbm, out_hbm,
-    lev, edges, halo, ready, recv, noise, cells, values, error, count, pick, target, observed, tall, packed,
-    row_sem, load_sem, halo_send, halo_recv, part_send, part_recv, own_sem, out_sem,
+    members_hbm, count_hbm, cells_hbm, values_hbm, error_hbm, noise_hbm, out,
+    lev, edges, halo, ready, recv, noise, cells, values, error, count, pick, target, observed, tall,
+    row_sem, load_sem, halo_send, halo_recv, part_send, part_recv, own_sem,
 ):
     fields, ens, rows, cols = members_hbm.shape
     waves = rows
@@ -109,10 +105,15 @@
     full = parts * ens
     slots = cells.shape[1]
     me = lax.axis_index("mem")
-    after, before = neighbour_ids()
+    total = lax.axis_size("tile") * lax.axis_size("grp")
+    slab = lax.axis_index("tile") * lax.axis_size("grp") + lax.axis_index("grp")
+    after, before = lax.rem(slab + 1, total), lax.rem(slab + total - 1, total)
     peers = [lax.rem(me + p, parts) for p in range(1, parts)]
-    targets = [after, before] + [{"mem": p} for p in peers]
+    targets = [place_of(after), place_of(before)] + [{"mem": p} for p in peers]
     quick = 1 - lax.rem(lax.axis_index("grp"), 2)
+    barrier = pltpu.get_barrier_semaphore()
+    for target_id in targets:
+        pl.semaphore_signal(barrier, inc=1, device_id=target_id, device_id_type=MESH)
 
     def row_load(r):
         return pltpu.make_async_copy(members_hbm.at[:, :, r, :], lev.at[STEPS + r], row_sem.at[r])
@@ -128,9 +129,6 @@
         row_load(k).start()
     for load in small:
         load.start()
-    barrier = pltpu.get_barrier_semaphore()
-    for target_id in targets:
-        pl.semaphore_signal(barrier, inc=1, device_id=target_id, device_id_type=MESH)
 
     def halo_copy(way, k):
         return pltpu.make_async_remote_copy(
@@ -138,18 +136,23 @@
             dst_ref=halo.at[way, k],
             send_sem=halo_send.at[way, k],
             recv_sem=halo_recv.at[way, k],
-            device_id=(after, before)[way],
+            device_id=place_of(after + way * (before - after)),
             device_id_type=MESH,
         )
 
+    patient = slab == (1 - quick) + quick * (total - 2)
     for k in range(STEPS):
         for way, r in ((0, rows - 1 - k), (1, k)):
             row_load(r).wait()
             edges[way, k] = lev[STEPS + r].astype(jnp.bfloat16)
         if k == 0:
             pl.semaphore_wait(barrier, len(targets))
-        for way in range(2):
-            halo_copy(way, k).start()
+
+        @pl.when(jnp.logical_not(patient))
+        def _():
+            halo_copy(quick, k).start()
+
+        halo_copy(1 - quick, k).start()
 
     def stencil(base, half):
         def at(i):
@@ -159,10 +162,10 @@
 
     def step_row(level, line):
         base = level * lines + line
-        for half in range(0, ens, 8):
-            done = stencil(base, half)
+        for m in range(0, ens, 8):
+            done = stencil(base, m)
             for f in range(fields):
-                lev[base + lines, f, pl.ds(half, 8), :] = done[f]
+                lev[base + lines, f, pl.ds(m, 8), :] = done[f]
 
     for level in range(STEPS - 1):
 
@@ -172,6 +175,11 @@
 
         lax.fori_loop(0, rows - 2 * (level + 1), inner_row, 0)
 
+    @pl.when(patient)
+    def _():
+        for k in range(STEPS):
+            halo_copy(quick, k).start()
+
     def wave_side(w):
         late = w // STEPS
         return quick + late - 2 * quick * late, lax.rem(w, STEPS)
@@ -180,13 +188,12 @@
         side, k = wave_side(w)
         return (STEPS - 1 - k) + side * (2 * k + 1)
 
-    def part_copy(w, kind, p):
-        f, number = ((0, 1), (1, fields - 1))[kind]
+    def part_copy(w, p):
         return pltpu.make_async_remote_copy(
-            src_ref=ready.at[w, peers[p], pl.ds(f, number)],
-            dst_ref=recv.at[w, pl.ds(f, number), pl.ds(me * ens, ens)],
-            send_sem=part_send.at[w, kind, p],
-            recv_sem=part_recv.at[w, kind, p],
+            src_ref=ready.at[w, peers[p]],
+            dst_ref=recv.at[w, :, pl.ds(me * ens, ens)],
+            send_sem=part_send.at[w, p],
+            recv_sem=part_recv.at[w, p],
             device_id={"mem": peers[p]},
             device_id_type=MESH,
         )
@@ -198,7 +205,7 @@
         side, k = wave_side(w)
         sign = 1 - 2 * side
         start = (STEPS - 1 - k) + side * (2 * k + lines - 2 * STEPS + 1)
-        pltpu.make_async_copy(halo.at[side, k], halo.at[side, k], halo_recv.at[side, k]).wait()
+        halo_copy(side, k).wait_recv()
         lev[start] = halo[side, k].astype(jnp.float32)
 
         def up(level, c):
@@ -213,9 +220,8 @@
                 both = jnp.concatenate([pair[0][f], pair[1][f]], axis=0).astype(jnp.bfloat16)
                 for d in range(parts):
                     ready[w, d, f, pl.ds(m, 16), :] = both[:, d * tile_cols : (d + 1) * tile_cols]
-        for kind in range(2):
-            for p in range(parts - 1):
-                part_copy(w, kind, p).start()
+        for p in range(parts - 1):
+            part_copy(w, p).start()
         own_copy(w).start()
         return carry
 
@@ -235,7 +241,7 @@
     chunk = 256 if slots % 256 == 0 else slots
     for s in range(0, slots, chunk):
         cut = slice(s, s + chunk)
-        for i, third in enumerate(split(values[:, cut] + error[:, cut] * noise[cut, :].T)):
+        for i, third in enumerate(split(values[:, cut] + error[:, cut] * noise[cut, :].T)[:2]):
             target[i, :, cut] = third
 
     lax.fori_loop(STEPS, waves, wave, 0)
@@ -243,7 +249,7 @@
     def arrived(w):
         own_copy(w).wait()
         for p in range(parts - 1):
-            part_copy(w, 0, p).wait_recv()
+            part_copy(w, p).wait_recv()
 
     def look(first, number, cut):
         seen = jnp.concatenate([recv[w, 0] for w in range(first, first + number)], axis=1)
@@ -264,17 +270,16 @@
         spread = yb - jnp.sum(yb, axis=0, keepdims=True) * (1.0 / full)
         wh, wm, wl = split(spread * weights[:, cut])
         yb = yb.astype(jnp.bfloat16)
-        dh, dm, dl = (target[i, :, cut] for i in range(3))
+        dh, dm = (target[i, :, cut] for i in range(2))
 
         def turned(a, b):
             return lax.dot_general(a, b, (((1,), (1,)), ((), ())), preferred_element_type=jnp.float32)
 
         one = turned(jnp.concatenate([yb, dh, dm], axis=0), jnp.concatenate([wh, wm], axis=0))
-        two = turned(jnp.concatenate([yb, dh], axis=0), wl)
-        three = turned(dl, wh)
-        term = [one[:full, :full], one[:full, full:] + two[:full]]
+        two = turned(yb, wl)
+        term = [one[:full, :full], one[:full, full:] + two]
         term += [one[full : 2 * full, :full]]
-        term += [one[full : 2 * full, full:] + one[2 * full :, :full] + one[2 * full :, full:] + two[full:] + three]
+        term += [one[full : 2 * full, full:] + one[2 * full :, :full] + one[2 * full :, full:]]
         both = term if both is None else [a + b for a, b in zip(both, term)]
     plain = both[0] + both[1]
     aimed = both[2] + both[3]
@@ -292,33 +297,29 @@
     mix = jnp.concatenate([upper, lower], axis=1)
     for f in range(fields):
         for w in range(0, waves, 2):
-            if f == 1:
-                for i in (w, w + 1):
-                    for p in range(parts - 1):
-                        part_copy(i, 1, p).wait_recv()
             block = jnp.concatenate([recv[w, f], recv[w + 1, f]], axis=1)
             done = mxu(mix, jnp.concatenate([block, block], axis=0))
             for i in range(2):
                 tall[f, pl.ds(wave_row(w + i), full, stride=rows), :] = done[:, i * tile_cols : (i + 1) * tile_cols]
-        packed[f] = tall[f].reshape(full, rows, tile_cols).astype(jnp.bfloat16)
-        pltpu.make_async_copy(packed.at[f], out_hbm.at[f], out_sem.at[f]).start()
+        out[f] = tall[f].reshape(full, rows, tile_cols).astype(jnp.bfloat16)
     for way in range(2):
         for k in range(STEPS):
             halo_copy(way, k).wait_send()
 
     def finish(w, carry):
-        for kind in range(2):
-            for p in range(parts - 1):
-                part_copy(w, kind, p).wait_send()
+        for p in range(parts - 1):
+            part_copy(w, p).wait_send()
         return carry
 
     lax.fori_loop(0, waves, finish, 0)
-    for f in range(fields):
-        pltpu.make_async_copy(packed.at[f], out_hbm.at[f], out_sem.at[f]).wait()
 
 
 def hbm():
     return pl.BlockSpec(memory_space=pltpu.HBM)
+
+
+def stay(q):
+    return pltpu.with_memory_space_constraint(q, pltpu.HBM)
 
 
 def body(members, obs_cells, obs_count, obs_values, obs_error, obs_noise):
@@ -337,7 +338,7 @@
         name="assimilate",
         out_shape=jax.ShapeDtypeStruct((fields, full, rows, tile_cols), jnp.bfloat16),
         in_specs=[hbm()] * 6,
-        out_specs=hbm(),
+        out_specs=pl.BlockSpec(memory_space=pltpu.VMEM),
         scratch_shapes=[
             pltpu.VMEM((STEPS * lines, fields, ens, cols), jnp.float32),
             edge,
@@ -350,23 +351,21 @@
             row,
             pltpu.VMEM((1, 1), jnp.int32),
             pltpu.VMEM((points, slots), jnp.bfloat16),
-            pltpu.VMEM((3, full, slots), jnp.bfloat16),
+            pltpu.VMEM((2, full, slots), jnp.bfloat16),
             pltpu.VMEM((full, slots), jnp.float32),
             pltpu.VMEM((fields, full * rows, tile_cols), jnp.float32),
-            pltpu.VMEM((fields, full, rows, tile_cols), jnp.bfloat16),
             dma((rows,)),
             dma((5,)),
             dma((2, STEPS)),
             dma((2, STEPS)),
-            dma((rows, 2, parts - 1)),
-            dma((rows, 2, parts - 1)),
+            dma((rows, parts - 1)),
+            dma((rows, parts - 1)),
             dma((rows,)),
-            dma((fields,)),
         ],
         compiler_params=pltpu.CompilerParams(
             vmem_limit_bytes=VMEM_BYTES, collective_id=0, has_side_effects=True
         ),
-    )(members, obs_count, obs_cells[0], obs_values[0], obs_error[0], obs_noise[0, 0])
+    )(stay(members), obs_count, *[stay(q) for q in (obs_cells[0], obs_values[0], obs_error[0], obs_noise[0, 0])])
 
 
 def solution(mesh):

time: 29.8 us -> 25.8 us (0.87)
  Pallas kernels: 26.9 us -> 24 us
  local copies, waits for them, and re-layouts: 2.06 us -> 0.88 us
    pallas_call x1, Pallas kernels: 26.9 us -> 24 us  [body(): pl.pallas_call(kernel, name='assimilate', out_shape=jax.ShapeDtypeStruct(...]
    unnamed x1, local copies, waits for them, and re-layouts: 2.06 us -> 0.88 us
where the time goes in v1:
time: 25.8 us; the launch traced here: 25.5 us
  Pallas kernels  24 us (93%)
  local copies, waits for them, and re-layouts  0.88 us (3%)
  between operations  0.66 us (3%)
    pallas_call x1, Pallas kernels, body(): pl.pallas_call(kernel, name='assimilate', out_shape=jax.ShapeDtypeStruct(...  24 us
    unnamed x1, local copies, waits for them, and re-layouts  0.88 us

profile of v1, /device:TPU:0, one launch (start us, length us, event | category | flops | bytes accessed | tf_op | source)
XLA Modules:
  0.0 25.5 jit_solution(6778781068732909839)
XLA Ops:
  0.7 24.0 %assimilate.1 = bf16[3,128,8,128]{3,2,1,0:T(8,128)(2,1)S(1)} custom-call(f32[3,32,8,512]{3,2,1,0:T(8,128)} %members_hbm.1, s32[1,1]{1,0:T(1,128)S(6)} %copy.8.count_hbm, s32[1,1024]{1,0:T(1,128)} %bitcast.5, f32[1,1024]{1,0:T(1,128)} %bitcast.6, f32[1,1024]{1,0:T(1,128)} %bitcast.7, f32[1024,128]{1,0:T(8,128)} %bitcast.4), custom_call_target="tpu_custom_call" | custom-call | tf_op jit(solution)/shard_map/assimilate/pallas_call | solution.py:336
  24.6 0.9 %copy.9 = bf16[3,128,8,128]{3,2,1,0:T(8,128)(2,1)} copy(bf16[3,128,8,128]{3,2,1,0:T(8,128)(2,1)S(1)} %assimilate.1) | data formatting | bytes 1572864

commit v2 on v1

--- a/solution.py
+++ b/solution.py
@@ -7,6 +7,7 @@
 
 STEPS = 4
 NEWTON_STEPS = 12
+LAST = 2
 
 courant = 0.3
 gravity = 1.0
@@ -38,6 +39,33 @@
         + (north(near - flux) + south(near + flux))
     )
     return new_h, new_u, new_v
+
+
+def known(mid, far, toward):
+    (h, u, v), (hf, uf, vf) = mid, far
+    cols = h.shape[1]
+    north = lambda q: pltpu.roll(q, cols - 1, 1)
+    south = lambda q: pltpu.roll(q, 1, 1)
+    flux = courant * (v + h * v)
+    near = 0.25 * h
+    new_h = 0.25 * hf - toward * (uf + hf * uf) + (north(near - flux) + south(near + flux))
+    un, us = north(u), south(u)
+    new_u = uf * (0.25 - (0.5 * toward) * uf) - (toward * gravity) * hf
+    new_u = new_u + (0.25 * (un + us) + v * (coriolis - courant * (un - us)))
+    flux = courant * (0.5 * (v * v) + gravity * h)
+    near = 0.25 * v
+    turn = toward * u
+    new_v = vf * (0.25 - turn) - coriolis * u + (north(near - flux) + south(near + flux))
+    return new_h, new_u, new_v, 0.25 + turn
+
+
+def joined(row, rest, toward):
+    (h, u, v), (rest_h, rest_u, rest_v, turn) = row, rest
+    return (
+        rest_h + (0.25 * h + toward * (u + h * u)),
+        rest_u + (u * (0.25 + (0.5 * toward) * u) + (toward * gravity) * h),
+        rest_v + v * turn,
+    )
 
 
 def split(q):
@@ -94,7 +122,7 @@
 
 def kernel(
     members_hbm, count_hbm, cells_hbm, values_hbm, error_hbm, noise_hbm, out,
-    lev, edges, halo, ready, recv, noise, cells, values, error, count, pick, target, observed, tall,
+    lev, edges, halo, ready, recv, partial, noise, cells, values, error, count, pick, target, wanted, heavy, tall,
     row_sem, load_sem, halo_send, halo_recv, part_send, part_recv, own_sem,
 ):
     fields, ens, rows, cols = members_hbm.shape
@@ -104,6 +132,7 @@
     parts, tile_cols = ready.shape[1], ready.shape[4]
     full = parts * ens
     slots = cells.shape[1]
+    points = rows * tile_cols
     me = lax.axis_index("mem")
     total = lax.axis_size("tile") * lax.axis_size("grp")
     slab = lax.axis_index("tile") * lax.axis_size("grp") + lax.axis_index("grp")
@@ -174,11 +203,12 @@
             return carry
 
         lax.fori_loop(0, rows - 2 * (level + 1), inner_row, 0)
-
-    @pl.when(patient)
-    def _():
-        for k in range(STEPS):
-            halo_copy(quick, k).start()
+        if level == 0:
+            @pl.when(patient)
+            def _():
+                for k in range(STEPS):
+                    halo_copy(quick, k).start()
+
 
     def wave_side(w):
         late = w // STEPS
@@ -188,12 +218,14 @@
         side, k = wave_side(w)
         return (STEPS - 1 - k) + side * (2 * k + 1)
 
-    def part_copy(w, p):
+    def part_copy(w, p, kind=0):
+        here = ((0, fields), (0, 1), (1, fields - 1))[kind]
+        slot = w + kind // 2 * LAST
         return pltpu.make_async_remote_copy(
-            src_ref=ready.at[w, peers[p]],
-            dst_ref=recv.at[w, :, pl.ds(me * ens, ens)],
-            send_sem=part_send.at[w, p],
-            recv_sem=part_recv.at[w, p],
+            src_ref=ready.at[w, peers[p], pl.ds(*here)],
+            dst_ref=recv.at[w, pl.ds(*here), pl.ds(me * ens, ens)],
+            send_sem=part_send.at[slot, p],
+            recv_sem=part_recv.at[slot, p],
             device_id={"mem": peers[p]},
             device_id_type=MESH,
         )
@@ -201,10 +233,18 @@
     def own_copy(w):
         return pltpu.make_async_copy(ready.at[w, me], recv.at[w, :, pl.ds(me * ens, ens)], own_sem.at[w])
 
+    def place(w):
+        side, k = wave_side(w)
+        return side, k, 1 - 2 * side, (STEPS - 1 - k) + side * (2 * k + lines - 2 * STEPS + 1)
+
+    def make_ready(w, m, pair):
+        for f in range(fields):
+            both = jnp.concatenate([pair[0][f], pair[1][f]], axis=0).astype(jnp.bfloat16)
+            for d in range(parts):
+                ready[w, d, f, pl.ds(m, 16), :] = both[:, d * tile_cols : (d + 1) * tile_cols]
+
     def wave(w, carry):
-        side, k = wave_side(w)
-        sign = 1 - 2 * side
-        start = (STEPS - 1 - k) + side * (2 * k + lines - 2 * STEPS + 1)
+        side, k, sign, start = place(w)
         halo_copy(side, k).wait_recv()
         lev[start] = halo[side, k].astype(jnp.float32)
 
@@ -215,17 +255,60 @@
         lax.fori_loop(0, STEPS - 1, up, 0)
         base = (STEPS - 1) * lines + start + sign * STEPS
         for m in range(0, ens, 16):
-            pair = [stencil(base, m), stencil(base, m + 8)]
-            for f in range(fields):
-                both = jnp.concatenate([pair[0][f], pair[1][f]], axis=0).astype(jnp.bfloat16)
-                for d in range(parts):
-                    ready[w, d, f, pl.ds(m, 16), :] = both[:, d * tile_cols : (d + 1) * tile_cols]
+            make_ready(w, m, [stencil(base, m), stencil(base, m + 8)])
         for p in range(parts - 1):
             part_copy(w, p).start()
         own_copy(w).start()
         return carry
 
+    def late_wave(w, kind, last=False):
+        side, k, sign, start = place(w)
+        toward = courant * sign.astype(jnp.float32)
+
+        def prepare(level, c):
+            base = level * lines + start + sign * (level + 1)
+            for m in range(0, ens, 8):
+                mid, far = ([lev[i, f, pl.ds(m, 8), :] for f in range(fields)] for i in (base, base + sign))
+                for i, q in enumerate(known(mid, far, toward)):
+                    partial[level, i, pl.ds(m, 8), :] = q
+            return c
+
+        lax.fori_loop(0, STEPS, prepare, 0)
+        halo_copy(side, k).wait_recv()
+        for m in range(0, ens, 16):
+            rows16 = [halo[side, k, f, pl.ds(m, 16), :].astype(jnp.float32) for f in range(fields)]
+            pair = []
+            for half in range(2):
+                now = [q[8 * half : 8 * half + 8] for q in rows16]
+                here = pl.ds(m + 8 * half, 8)
+                for level in range(STEPS):
+                    if not last:
+                        for f in range(fields):
+                            lev[level * lines + start + sign * level, f, here, :] = now[f]
+                    now = joined(now, [partial[level, i, here, :] for i in range(fields + 1)], toward)
+                pair.append(now)
+            make_ready(w, m, pair)
+        for p in range(parts - 1):
+            part_copy(w, p, kind).start()
+        own_copy(w).start()
+
+    def late_loop(w, carry):
+        late_wave(w, 0)
+        return carry
+
     lax.fori_loop(0, STEPS, wave, 0)
+
+    lax.fori_loop(STEPS, waves - LAST, late_loop, 0)
+    for w in range(waves - LAST, waves):
+        late_wave(w, 1, w == waves - 1)
+    for w in range(waves - LAST, waves):
+        for p in range(parts - 1):
+            part_copy(w, p, 2).start()
+
+    def arrived(w):
+        own_copy(w).wait()
+        for p in range(parts - 1):
+            part_copy(w, p, 1 if w >= waves - LAST else 0).wait_recv()
 
     for load in small:
         load.wait()
@@ -238,51 +321,49 @@
         return carry
 
     lax.fori_loop(0, waves, select, 0)
+    slot_ids = lax.broadcasted_iota(jnp.int32, (1, slots), 1)
+    weights = jnp.where(slot_ids < count[...], 1.0 / (error[...] * error[...]), 0.0)
     chunk = 256 if slots % 256 == 0 else slots
     for s in range(0, slots, chunk):
         cut = slice(s, s + chunk)
-        for i, third in enumerate(split(values[:, cut] + error[:, cut] * noise[cut, :].T)[:2]):
-            target[i, :, cut] = third
-
-    lax.fori_loop(STEPS, waves, wave, 0)
-
-    def arrived(w):
-        own_copy(w).wait()
-        for p in range(parts - 1):
-            part_copy(w, p).wait_recv()
-
-    def look(first, number, cut):
+        asked = weights[:, cut] * (values[:, cut] + error[:, cut] * noise[cut, :].T)
+        for i, third in enumerate(split(asked)[:2]):
+            target[i * full : (i + 1) * full, cut] = third
+    line_ids = lax.broadcasted_iota(jnp.int32, (16, slots), 0)
+    thirds = [q.astype(jnp.float32) for q in split(weights)]
+    target[2 * full :, :] = jnp.where(
+        line_ids == 0, thirds[0], jnp.where(line_ids == 1, thirds[1], jnp.where(line_ids == 2, thirds[2], 0.0))
+    ).astype(jnp.bfloat16)
+
+    def turned(a, b):
+        return lax.dot_general(a, b, (((1,), (1,)), ((), ())), preferred_element_type=jnp.float32)
+
+    chunk = 2 * tile_cols
+    for c in range(0, points, chunk):
+        cut = slice(c, c + chunk)
+        summed = turned(target[...], pick[cut, :])
+        for i, third in enumerate(split(summed[:full] + summed[full : 2 * full])[:2]):
+            wanted[i * full : (i + 1) * full, cut] = third
+        tail = summed[2 * full :]
+        heavy[:, cut] = tail[0:1] + (tail[1:2] + tail[2:3])
+
+    def observe(first, number):
+        cut = slice(first * tile_cols, (first + number) * tile_cols)
         seen = jnp.concatenate([recv[w, 0] for w in range(first, first + number)], axis=1)
-        return mxu(seen, pick[first * tile_cols : (first + number) * tile_cols, cut])
+        near = seen.astype(jnp.float32)
+        spread = near - jnp.sum(near, axis=0, keepdims=True) * (1.0 / full)
+        wh, wm, wl = split(spread * heavy[:, cut])
+        one = turned(seen, jnp.concatenate([wh, wm], axis=0))
+        plain = one[:, :full] + (one[:, full:] + turned(seen, wl))
+        two = turned(wanted[:, cut], seen)
+        return plain, two[:full] + two[full:]
 
     early = waves - 1
     for w in range(early):
         arrived(w)
-    for s in range(0, slots, chunk):
-        observed[:, s : s + chunk] = look(0, early, slice(s, s + chunk))
+    plain, aimed = observe(0, early)
     arrived(early)
-    slot_ids = lax.broadcasted_iota(jnp.int32, (1, slots), 1)
-    weights = jnp.where(slot_ids < count[...], 1.0 / (error[...] * error[...]), 0.0)
-    both = None
-    for s in range(0, slots, chunk):
-        cut = slice(s, s + chunk)
-        yb = observed[:, cut] + look(early, 1, cut)
-        spread = yb - jnp.sum(yb, axis=0, keepdims=True) * (1.0 / full)
-        wh, wm, wl = split(spread * weights[:, cut])
-        yb = yb.astype(jnp.bfloat16)
-        dh, dm = (target[i, :, cut] for i in range(2))
-
-        def turned(a, b):
-            return lax.dot_general(a, b, (((1,), (1,)), ((), ())), preferred_element_type=jnp.float32)
-
-        one = turned(jnp.concatenate([yb, dh, dm], axis=0), jnp.concatenate([wh, wm], axis=0))
-        two = turned(yb, wl)
-        term = [one[:full, :full], one[:full, full:] + two]
-        term += [one[full : 2 * full, :full]]
-        term += [one[full : 2 * full, full:] + one[2 * full :, :full] + one[2 * full :, full:]]
-        both = term if both is None else [a + b for a, b in zip(both, term)]
-    plain = both[0] + both[1]
-    aimed = both[2] + both[3]
+    plain, aimed = (a + b for a, b in zip((plain, aimed), observe(early, 1)))
     least = full - 1.0
     eye = jnp.where(
         lax.broadcasted_iota(jnp.int32, (full, full), 0) == lax.broadcasted_iota(jnp.int32, (full, full), 1), 1.0, 0.0
@@ -297,6 +378,11 @@
     mix = jnp.concatenate([upper, lower], axis=1)
     for f in range(fields):
         for w in range(0, waves, 2):
+            if f == 1:
+                for i in (w, w + 1):
+                    if i >= waves - LAST:
+                        for p in range(parts - 1):
+                            part_copy(i, p, 2).wait_recv()
             block = jnp.concatenate([recv[w, f], recv[w + 1, f]], axis=1)
             done = mxu(mix, jnp.concatenate([block, block], axis=0))
             for i in range(2):
@@ -311,7 +397,11 @@
             part_copy(w, p).wait_send()
         return carry
 
-    lax.fori_loop(0, waves, finish, 0)
+    lax.fori_loop(0, waves - LAST, finish, 0)
+    for w in range(waves - LAST, waves):
+        for kind in (1, 2):
+            for p in range(parts - 1):
+                part_copy(w, p, kind).wait_send()
 
 
 def hbm():
@@ -345,21 +435,23 @@
             edge,
             pltpu.VMEM((rows, parts, fields, ens, tile_cols), jnp.bfloat16),
             pltpu.VMEM((rows, fields, full, tile_cols), jnp.bfloat16),
+            pltpu.VMEM((STEPS, fields + 1, ens, cols), jnp.float32),
             pltpu.VMEM(obs_noise.shape[2:], jnp.float32),
             pltpu.VMEM((1, slots), jnp.int32),
             row,
             row,
             pltpu.VMEM((1, 1), jnp.int32),
             pltpu.VMEM((points, slots), jnp.bfloat16),
-            pltpu.VMEM((2, full, slots), jnp.bfloat16),
-            pltpu.VMEM((full, slots), jnp.float32),
+            pltpu.VMEM((2 * full + 16, slots), jnp.bfloat16),
+            pltpu.VMEM((2 * full, points), jnp.bfloat16),
+            pltpu.VMEM((1, points), jnp.float32),
             pltpu.VMEM((fields, full * rows, tile_cols), jnp.float32),
             dma((rows,)),
             dma((5,)),
             dma((2, STEPS)),
             dma((2, STEPS)),
-            dma((rows, parts - 1)),
-            dma((rows, parts - 1)),
+            dma((rows + LAST, parts - 1)),
+            dma((rows + LAST, parts - 1)),
             dma((rows,)),
         ],
         compiler_params=pltpu.CompilerParams(

time: 25.8 us -> 23.9 us (0.926)
  Pallas kernels: 24 us -> 22.2 us
    pallas_call x1, Pallas kernels: 24 us -> 22.2 us  [body(): pl.pallas_call(kernel, name='assimilate', out_shape=jax.ShapeDtypeStruct(...]
where the time goes in v2:
time: 23.9 us; the launch traced here: 23.7 us
  Pallas kernels  22.2 us (93%)
  local copies, waits for them, and re-layouts  0.88 us (4%)
  between operations  0.66 us (3%)
    pallas_call x1, Pallas kernels, body(): pl.pallas_call(kernel, name='assimilate', out_shape=jax.ShapeDtypeStruct(...  22.2 us
    unnamed x1, local copies, waits for them, and re-layouts  0.88 us

profile of v2, /device:TPU:0, one launch (start us, length us, event | category | flops | bytes accessed | tf_op | source)
XLA Modules:
  0.0 23.7 jit_solution(4536221316193943614)
XLA Ops:
  0.7 22.2 %assimilate.1 = bf16[3,128,8,128]{3,2,1,0:T(8,128)(2,1)S(1)} custom-call(f32[3,32,8,512]{3,2,1,0:T(8,128)} %members_hbm.1, s32[1,1]{1,0:T(1,128)S(6)} %copy.8.count_hbm, s32[1,1024]{1,0:T(1,128)} %bitcast.5, f32[1,1024]{1,0:T(1,128)} %bitcast.6, f32[1,1024]{1,0:T(1,128)} %bitcast.7, f32[1024,128]{1,0:T(8,128)} %bitcast.4), custom_call_target="tpu_custom_call" | custom-call | tf_op jit(solution)/shard_map/assimilate/pallas_call | solution.py:426
  22.8 0.9 %copy.9 = bf16[3,128,8,128]{3,2,1,0:T(8,128)(2,1)} copy(bf16[3,128,8,128]{3,2,1,0:T(8,128)(2,1)S(1)} %assimilate.1) | data formatting | bytes 1572864

commit v3 on v2

--- a/solution.py
+++ b/solution.py
@@ -6,7 +6,7 @@
 from jax.sharding import PartitionSpec as P
 
 STEPS = 4
-NEWTON_STEPS = 12
+NEWTON_STEPS = 11
 LAST = 2
 
 courant = 0.3
@@ -79,13 +79,15 @@
     return jnp.dot(a, b, preferred_element_type=jnp.float32)
 
 
-def product(a, b):
+def product(a, b, fine=True):
     (ah, am, al), (bh, bm, bl) = a, b
     size = bh.shape[1]
     top = mxu(
         jnp.concatenate([ah, am], axis=1),
         jnp.concatenate([jnp.concatenate([bh, bm], axis=1)] * 2, axis=0),
     )
+    if not fine:
+        return top[:, :size] + top[:, size:]
     low = mxu(jnp.concatenate([ah, al], axis=1), jnp.concatenate([bl, bh], axis=0))
     return top[:, :size] + (top[:, size:] + low)
 
@@ -100,19 +102,19 @@
     )
     low = least * scale
     y, x = gram * scale, eye * scale
-    for _ in range(NEWTON_STEPS):
+    for step in range(NEWTON_STEPS):
         mid = 1.0 + low
         gain = 4.0 / (mid * mid)
         low = gain * low
         parts = split(y)
         both = [jnp.concatenate(pair, axis=0) for pair in zip(parts, split(x))]
-        done = product(both, parts)
+        done = product(both, parts, step < NEWTON_STEPS - 4)
         y = gain * (mid * y - done[:size])
         x = gain * (mid * x - done[size:])
     inverse = split(x)
-    found = product(split(rhs), inverse)
+    found = product(split(rhs), inverse, False)
     rest = rhs - product(split(found), split(gram))
-    return found + product(split(rest), inverse), eye
+    return found + product(split(rest), inverse, False), eye
 
 
 def place_of(slab):
@@ -123,7 +125,7 @@
 def kernel(
     members_hbm, count_hbm, cells_hbm, values_hbm, error_hbm, noise_hbm, out,
     lev, edges, halo, ready, recv, partial, noise, cells, values, error, count, pick, target, wanted, heavy, tall,
-    row_sem, load_sem, halo_send, halo_recv, part_send, part_recv, own_sem,
+    row_sem, load_sem, halo_send, halo_recv, part_send, part_recv,
 ):
     fields, ens, rows, cols = members_hbm.shape
     waves = rows
@@ -163,7 +165,7 @@
         return pltpu.make_async_remote_copy(
             src_ref=edges.at[way, k],
             dst_ref=halo.at[way, k],
-            send_sem=halo_send.at[way, k],
+            send_sem=halo_send,
             recv_sem=halo_recv.at[way, k],
             device_id=place_of(after + way * (before - after)),
             device_id_type=MESH,
@@ -218,20 +220,25 @@
         side, k = wave_side(w)
         return (STEPS - 1 - k) + side * (2 * k + 1)
 
-    def part_copy(w, p, kind=0):
-        here = ((0, fields), (0, 1), (1, fields - 1))[kind]
-        slot = w + kind // 2 * LAST
-        return pltpu.make_async_remote_copy(
-            src_ref=ready.at[w, peers[p], pl.ds(*here)],
-            dst_ref=recv.at[w, pl.ds(*here), pl.ds(me * ens, ens)],
-            send_sem=part_send.at[slot, p],
-            recv_sem=part_recv.at[slot, p],
-            device_id={"mem": peers[p]},
-            device_id_type=MESH,
-        )
-
-    def own_copy(w):
-        return pltpu.make_async_copy(ready.at[w, me], recv.at[w, :, pl.ds(me * ens, ens)], own_sem.at[w])
+    def span(w, kind):
+        return pl.ds(*((0, fields), (0, 1), (1, fields - 1))[kind]), part_recv.at[w + kind // 2 * LAST]
+
+    def part_start(w, kind):
+        here, landed = span(w, kind)
+        for peer in peers:
+            pltpu.make_async_remote_copy(
+                src_ref=ready.at[w, peer, here],
+                dst_ref=recv.at[w, here, pl.ds(me * ens, ens)],
+                send_sem=part_send,
+                recv_sem=landed,
+                device_id={"mem": peer},
+                device_id_type=MESH,
+            ).start()
+        pltpu.make_async_copy(ready.at[w, me, here], recv.at[w, here, pl.ds(me * ens, ens)], landed).start()
+
+    def arrived(w, kind):
+        here, landed = span(w, kind)
+        pltpu.make_async_copy(recv.at[w, here], recv.at[w, here], landed).wait()
 
     def place(w):
         side, k = wave_side(w)
@@ -256,9 +263,7 @@
         base = (STEPS - 1) * lines + start + sign * STEPS
         for m in range(0, ens, 16):
             make_ready(w, m, [stencil(base, m), stencil(base, m + 8)])
-        for p in range(parts - 1):
-            part_copy(w, p).start()
-        own_copy(w).start()
+        part_start(w, 0)
         return carry
 
     def late_wave(w, kind, last=False):
@@ -288,9 +293,7 @@
                     now = joined(now, [partial[level, i, here, :] for i in range(fields + 1)], toward)
                 pair.append(now)
             make_ready(w, m, pair)
-        for p in range(parts - 1):
-            part_copy(w, p, kind).start()
-        own_copy(w).start()
+        part_start(w, kind)
 
     def late_loop(w, carry):
         late_wave(w, 0)
@@ -302,13 +305,7 @@
     for w in range(waves - LAST, waves):
         late_wave(w, 1, w == waves - 1)
     for w in range(waves - LAST, waves):
-        for p in range(parts - 1):
-            part_copy(w, p, 2).start()
-
-    def arrived(w):
-        own_copy(w).wait()
-        for p in range(parts - 1):
-            part_copy(w, p, 1 if w >= waves - LAST else 0).wait_recv()
+        part_start(w, 2)
 
     for load in small:
         load.wait()
@@ -360,9 +357,9 @@
 
     early = waves - 1
     for w in range(early):
-        arrived(w)
+        arrived(w, 1 if w >= waves - LAST else 0)
     plain, aimed = observe(0, early)
-    arrived(early)
+    arrived(early, 1)
     plain, aimed = (a + b for a, b in zip((plain, aimed), observe(early, 1)))
     least = full - 1.0
     eye = jnp.where(
@@ -381,27 +378,15 @@
             if f == 1:
                 for i in (w, w + 1):
                     if i >= waves - LAST:
-                        for p in range(parts - 1):
-                            part_copy(i, p, 2).wait_recv()
+                        arrived(i, 2)
             block = jnp.concatenate([recv[w, f], recv[w + 1, f]], axis=1)
             done = mxu(mix, jnp.concatenate([block, block], axis=0))
             for i in range(2):
                 tall[f, pl.ds(wave_row(w + i), full, stride=rows), :] = done[:, i * tile_cols : (i + 1) * tile_cols]
         out[f] = tall[f].reshape(full, rows, tile_cols).astype(jnp.bfloat16)
-    for way in range(2):
-        for k in range(STEPS):
-            halo_copy(way, k).wait_send()
-
-    def finish(w, carry):
-        for p in range(parts - 1):
-            part_copy(w, p).wait_send()
-        return carry
-
-    lax.fori_loop(0, waves - LAST, finish, 0)
-    for w in range(waves - LAST, waves):
-        for kind in (1, 2):
-            for p in range(parts - 1):
-                part_copy(w, p, kind).wait_send()
+    pltpu.make_async_copy(edges, edges, halo_send).wait()
+    gone = ready.at[:, pl.ds(0, parts - 1)]
+    pltpu.make_async_copy(gone, gone, part_send).wait()
 
 
 def hbm():
@@ -448,11 +433,10 @@
             pltpu.VMEM((fields, full * rows, tile_cols), jnp.float32),
             dma((rows,)),
             dma((5,)),
+            dma,
             dma((2, STEPS)),
-            dma((2, STEPS)),
-            dma((rows + LAST, parts - 1)),
-            dma((rows + LAST, parts - 1)),
-            dma((rows,)),
+            dma,
+            dma((rows + LAST,)),
         ],
         compiler_params=pltpu.CompilerParams(
             vmem_limit_bytes=VMEM_BYTES, collective_id=0, has_side_effects=True

time: 23.9 us -> 22.9 us (0.958)
  Pallas kernels: 22.2 us -> 21.2 us
    pallas_call x1, Pallas kernels: 22.2 us -> 21.2 us  [body(): pl.pallas_call(kernel, name='assimilate', out_shape=jax.ShapeDtypeStruct(...]
where the time goes in v3:
time: 22.9 us; the launch traced here: 22.8 us
  Pallas kernels  21.2 us (93%)
  local copies, waits for them, and re-layouts  0.88 us (4%)
  between operations  0.66 us (3%)
    pallas_call x1, Pallas kernels, body(): pl.pallas_call(kernel, name='assimilate', out_shape=jax.ShapeDtypeStruct(...  21.2 us
    unnamed x1, local copies, waits for them, and re-layouts  0.88 us

profile of v3, /device:TPU:0, one launch (start us, length us, event | category | flops | bytes accessed | tf_op | source)
XLA Modules:
  0.0 22.8 jit_solution(6014494240777364699)
XLA Ops:
  0.7 21.2 %assimilate.1 = bf16[3,128,8,128]{3,2,1,0:T(8,128)(2,1)S(1)} custom-call(f32[3,32,8,512]{3,2,1,0:T(8,128)} %members_hbm.1, s32[1,1]{1,0:T(1,128)S(6)} %copy.8.count_hbm, s32[1,1024]{1,0:T(1,128)} %bitcast.5, f32[1,1024]{1,0:T(1,128)} %bitcast.6, f32[1,1024]{1,0:T(1,128)} %bitcast.7, f32[1024,128]{1,0:T(8,128)} %bitcast.4), custom_call_target="tpu_custom_call" | custom-call | tf_op jit(solution)/shard_map/assimilate/pallas_call | solution.py:411
  21.9 0.9 %copy.9 = bf16[3,128,8,128]{3,2,1,0:T(8,128)(2,1)} copy(bf16[3,128,8,128]{3,2,1,0:T(8,128)(2,1)S(1)} %assimilate.1) | data formatting | bytes 1572864

commit v4 on v3

--- a/solution.py
+++ b/solution.py
@@ -101,19 +101,28 @@
         lax.broadcasted_iota(jnp.int32, (size, size), 0) == lax.broadcasted_iota(jnp.int32, (size, size), 1), 1.0, 0.0
     )
     low = least * scale
-    y, x = gram * scale, eye * scale
-    for step in range(NEWTON_STEPS):
+    mid = 1.0 + low
+    gain = 4.0 / (mid * mid)
+    low = gain * low
+    first = split(gram)
+    y = (gain * mid * scale) * gram - (gain * scale * scale) * product(first, first)
+    x = (gain * mid * scale) * eye - (gain * scale * scale) * gram
+    for step in range(1, NEWTON_STEPS):
         mid = 1.0 + low
         gain = 4.0 / (mid * mid)
         low = gain * low
+        fine = step < NEWTON_STEPS - 4
         parts = split(y)
+        if step == NEWTON_STEPS - 1:
+            x = gain * (mid * x - product(split(x), parts, fine))
+            break
         both = [jnp.concatenate(pair, axis=0) for pair in zip(parts, split(x))]
-        done = product(both, parts, step < NEWTON_STEPS - 4)
+        done = product(both, parts, fine)
         y = gain * (mid * y - done[:size])
         x = gain * (mid * x - done[size:])
     inverse = split(x)
     found = product(split(rhs), inverse, False)
-    rest = rhs - product(split(found), split(gram))
+    rest = rhs - product(split(found), first)
     return found + product(split(rest), inverse, False), eye
 
 

time: 22.9 us -> 22.8 us (level)
  no operation moved by 1% of the time
where the time goes in v4:
time: 22.8 us; the launch traced here: 22.6 us
  Pallas kernels  21.1 us (93%)
  local copies, waits for them, and re-layouts  0.88 us (4%)
  between operations  0.66 us (3%)
    pallas_call x1, Pallas kernels, body(): pl.pallas_call(kernel, name='assimilate', out_shape=jax.ShapeDtypeStruct(...  21.1 us
    unnamed x1, local copies, waits for them, and re-layouts  0.88 us

profile of v4, /device:TPU:0, one launch (start us, length us, event | category | flops | bytes accessed | tf_op | source)
XLA Modules:
  0.0 22.6 jit_solution(13774463976091444113)
XLA Ops:
  0.7 21.1 %assimilate.1 = bf16[3,128,8,128]{3,2,1,0:T(8,128)(2,1)S(1)} custom-call(f32[3,32,8,512]{3,2,1,0:T(8,128)} %members_hbm.1, s32[1,1]{1,0:T(1,128)S(6)} %copy.8.count_hbm, s32[1,1024]{1,0:T(1,128)} %bitcast.5, f32[1,1024]{1,0:T(1,128)} %bitcast.6, f32[1,1024]{1,0:T(1,128)} %bitcast.7, f32[1024,128]{1,0:T(8,128)} %bitcast.4), custom_call_target="tpu_custom_call" | custom-call | tf_op jit(solution)/shard_map/assimilate/pallas_call | solution.py:420
  21.8 0.9 %copy.9 = bf16[3,128,8,128]{3,2,1,0:T(8,128)(2,1)} copy(bf16[3,128,8,128]{3,2,1,0:T(8,128)(2,1)S(1)} %assimilate.1) | data formatting | bytes 1572864

commit v5 on v4

--- a/solution.py
+++ b/solution.py
@@ -253,9 +253,9 @@
         side, k = wave_side(w)
         return side, k, 1 - 2 * side, (STEPS - 1 - k) + side * (2 * k + lines - 2 * STEPS + 1)
 
-    def make_ready(w, m, pair):
-        for f in range(fields):
-            both = jnp.concatenate([pair[0][f], pair[1][f]], axis=0).astype(jnp.bfloat16)
+    def make_ready(w, m, pair, some=None):
+        for i, f in enumerate(range(fields) if some is None else some):
+            both = jnp.concatenate([pair[0][i], pair[1][i]], axis=0).astype(jnp.bfloat16)
             for d in range(parts):
                 ready[w, d, f, pl.ds(m, 16), :] = both[:, d * tile_cols : (d + 1) * tile_cols]
 
@@ -289,6 +289,7 @@
 
         lax.fori_loop(0, STEPS, prepare, 0)
         halo_copy(side, k).wait_recv()
+        rests = []
         for m in range(0, ens, 16):
             rows16 = [halo[side, k, f, pl.ds(m, 16), :].astype(jnp.float32) for f in range(fields)]
             pair = []
@@ -301,8 +302,14 @@
                             lev[level * lines + start + sign * level, f, here, :] = now[f]
                     now = joined(now, [partial[level, i, here, :] for i in range(fields + 1)], toward)
                 pair.append(now)
-            make_ready(w, m, pair)
+            if last:
+                make_ready(w, m, [q[:1] for q in pair], (0,))
+                rests.append([q[1:] for q in pair])
+            else:
+                make_ready(w, m, pair)
         part_start(w, kind)
+        for i, pair in enumerate(rests):
+            make_ready(w, 16 * i, pair, (1, 2))
 
     def late_loop(w, carry):
         late_wave(w, 0)

time: 22.8 us -> 22.8 us (level)
  no operation moved by 1% of the time
where the time goes in v5:
time: 22.8 us; the launch traced here: 22.6 us
  Pallas kernels  21.1 us (93%)
  local copies, waits for them, and re-layouts  0.88 us (4%)
  between operations  0.66 us (3%)
    pallas_call x1, Pallas kernels, body(): pl.pallas_call(kernel, name='assimilate', out_shape=jax.ShapeDtypeStruct(...  21.1 us
    unnamed x1, local copies, waits for them, and re-layouts  0.88 us

profile of v5, /device:TPU:0, one launch (start us, length us, event | category | flops | bytes accessed | tf_op | source)
XLA Modules:
  0.0 22.6 jit_solution(15255891728096216356)
XLA Ops:
  0.7 21.1 %assimilate.1 = bf16[3,128,8,128]{3,2,1,0:T(8,128)(2,1)S(1)} custom-call(f32[3,32,8,512]{3,2,1,0:T(8,128)} %members_hbm.1, s32[1,1]{1,0:T(1,128)S(6)} %copy.8.count_hbm, s32[1,1024]{1,0:T(1,128)} %bitcast.5, f32[1,1024]{1,0:T(1,128)} %bitcast.6, f32[1,1024]{1,0:T(1,128)} %bitcast.7, f32[1024,128]{1,0:T(8,128)} %bitcast.4), custom_call_target="tpu_custom_call" | custom-call | tf_op jit(solution)/shard_map/assimilate/pallas_call | solution.py:427
  21.7 0.9 %copy.9 = bf16[3,128,8,128]{3,2,1,0:T(8,128)(2,1)} copy(bf16[3,128,8,128]{3,2,1,0:T(8,128)(2,1)S(1)} %assimilate.1) | data formatting | bytes 1572864

commit v6 on v4

--- a/solution.py
+++ b/solution.py
@@ -116,10 +116,7 @@
         if step == NEWTON_STEPS - 1:
             x = gain * (mid * x - product(split(x), parts, fine))
             break
-        both = [jnp.concatenate(pair, axis=0) for pair in zip(parts, split(x))]
-        done = product(both, parts, fine)
-        y = gain * (mid * y - done[:size])
-        x = gain * (mid * x - done[size:])
+        y, x = gain * (mid * y - product(parts, parts, fine)), gain * (mid * x - product(split(x), parts, fine))
     inverse = split(x)
     found = product(split(rhs), inverse, False)
     rest = rhs - product(split(found), first)

time: 22.8 us -> 22.8 us (level)
  no operation moved by 1% of the time
where the time goes in v6:
time: 22.8 us; the launch traced here: 22.7 us
  Pallas kernels  21.1 us (93%)
  local copies, waits for them, and re-layouts  0.88 us (4%)
  between operations  0.66 us (3%)
    pallas_call x1, Pallas kernels, body(): pl.pallas_call(kernel, name='assimilate', out_shape=jax.ShapeDtypeStruct(...  21.1 us
    unnamed x1, local copies, waits for them, and re-layouts  0.88 us

profile of v6, /device:TPU:0, one launch (start us, length us, event | category | flops | bytes accessed | tf_op | source)
XLA Modules:
  0.0 22.7 jit_solution(2554258515300712072)
XLA Ops:
  0.7 21.1 %assimilate.1 = bf16[3,128,8,128]{3,2,1,0:T(8,128)(2,1)S(1)} custom-call(f32[3,32,8,512]{3,2,1,0:T(8,128)} %members_hbm.1, s32[1,1]{1,0:T(1,128)S(6)} %copy.8.count_hbm, s32[1,1024]{1,0:T(1,128)} %bitcast.5, f32[1,1024]{1,0:T(1,128)} %bitcast.6, f32[1,1024]{1,0:T(1,128)} %bitcast.7, f32[1024,128]{1,0:T(8,128)} %bitcast.4), custom_call_target="tpu_custom_call" | custom-call | tf_op jit(solution)/shard_map/assimilate/pallas_call | solution.py:417
  21.8 0.9 %copy.9 = bf16[3,128,8,128]{3,2,1,0:T(8,128)(2,1)} copy(bf16[3,128,8,128]{3,2,1,0:T(8,128)(2,1)S(1)} %assimilate.1) | data formatting | bytes 1572864
